TPU v7x, 256 devices: a whole 4x4x8 slice. The times are simulated.
256 devices in a mesh: grp: 2 (over core), tok: 32 (over z, y), head: 4 (over x).
Axes of the slice: x: 4, y: 4, z: 8, core: 2. Of those that a mesh axis runs over, the one named last changes fastest.
Arguments:
- hidden_in: bfloat16 [2, 4096, 2560], P('grp', 'tok', 'head'), may hold values from -6 to 6
- attn_gain: bfloat16 [2560], replicated, may hold values from 0.5 to 1.5
- w_query: bfloat16 [2560, 2560], P('grp', 'head'), may hold values from -0.125 to 0.125
- key_projection_weight: bfloat16 [2560, 512], P('grp', 'head'), may hold values from -0.25 to 0.25
- value_projection_weight: bfloat16 [2560, 512], P('grp', 'head'), may hold values from -0.125 to 0.125
- w_out: bfloat16 [2560, 2560], P('grp', 'head'), may hold values from -0.125 to 0.125
- prefix_keys: bfloat16 [2, 2048, 4, 128], P('grp', 'tok', 'head'), may hold values from -91 to 91
- cached_prefix_values: bfloat16 [2, 2048, 4, 128], P('grp', 'tok', 'head'), may hold values from -6 to 6
- request_lengths: int32 [2, 16], P('grp'), may hold values from 1 to 1024, 4096 in all within a row
- moe_gain: bfloat16 [2560], replicated, may hold values from 0.5 to 1.5
- expert_ids: int32 [2, 4096, 6], P('grp', 'tok'), may hold values from 0 to 63, all different within a row; in each aligned block of 128 rows (0 to 127, 128 to 255, ..., all dimensions but the last counted through in order) at most 16 rows name the same one
- route_weights: float32 [2, 4096, 6], P('grp', 'tok'), may hold values from 0.05 to 0.3
- w_gate: bfloat16 [64, 2560, 1536], P(('grp', 'tok'), None, 'head'), may hold values from -0.125 to 0.125
- w_up: bfloat16 [64, 2560, 1536], P(('grp', 'tok'), None, 'head'), may hold values from -0.125 to 0.125
- w_down: bfloat16 [64, 1536, 2560], P(('grp', 'tok'), None, 'head'), may hold values from -0.15625 to 0.15625
Outputs:
- hidden_out: bfloat16 [2, 4096, 2560], P('grp', 'tok', 'head')
Inputs may be any that keep to these rules, and one draw needn't show every extreme that they name: `expert_ids`: each token names 6 different experts. Among the tokens of one device (aligned blocks of 128 tokens of a group) no expert is named more than 16 times.
All inputs are finite; a program needn't handle non-finite values.
Results may differ from a plain program's by a relative error of at most 0.011.
Values may be sent and summed in bfloat16 or wider, within the bound.
A program may use at most 64 MiB of HBM per device.

v0:
```python
import math
import jax
import jax.numpy as jnp
from jax import lax
from jax.sharding import PartitionSpec as P

ROPE_BASE = 500000.0
NORM_EPS = 1e-06
MASKED = -1e30


def shifted(block, axis, distance):
    devices = range(lax.axis_size(axis))
    route = [(i - distance, i) for i in devices if i - distance in devices]
    return lax.ppermute(block, axis, route)


def rms_norm(values_in, gain_vector):
    widened = values_in.astype(jnp.float32)
    mean_sq = jnp.mean(widened * widened, axis=-1, keepdims=True)
    return (widened * lax.rsqrt(mean_sq + NORM_EPS) * gain_vector.astype(jnp.float32)).astype(
        jnp.bfloat16
    )


def apply_rotary(product, token_positions):
    half_dim = product.shape[-1] // 2
    frequency = jnp.exp(
        jnp.arange(half_dim, dtype=jnp.float32) * (-2.0 * math.log(ROPE_BASE) / product.shape[-1])
    )
    angles = token_positions.astype(jnp.float32)[:, None] * frequency[None, :]
    cosine = jnp.cos(angles)[:, None, :]
    sine_part = jnp.sin(angles)[:, None, :]
    first_half = product[..., :half_dim]
    second_half = product[..., half_dim:]
    turned = jnp.concatenate(
        [
            first_half * cosine - second_half * sine_part,
            second_half * cosine + first_half * sine_part,
        ],
        axis=-1,
    )
    return turned.astype(jnp.bfloat16)


def attend(running, queries, keys_block, values_block, visible):
    row_max, row_total, summed = running
    scores = jnp.einsum(
        "tcrd,kcd->ctrk", queries, keys_block, preferred_element_type=jnp.float32
    ) * queries.shape[-1] ** (-0.5)
    if visible is not None:
        scores = jnp.where(visible[None, :, None, :], scores, MASKED)
    new_max = jnp.maximum(row_max, jnp.max(scores, axis=-1))
    weights = jnp.exp(scores - new_max[..., None])
    if visible is not None:
        weights = jnp.where(visible[None, :, None, :], weights, 0.0)
    factor = jnp.exp(row_max - new_max)
    row_total = row_total * factor + jnp.sum(weights, axis=-1)
    summed = summed * factor[..., None] + jnp.einsum(
        "ctrk,kcd->ctrd",
        weights.astype(jnp.bfloat16),
        values_block,
        preferred_element_type=jnp.float32,
    )
    return (new_max, row_total, summed)


def on_device(
    hidden_in,
    attn_gain,
    w_query,
    key_projection_weight,
    value_projection_weight,
    w_out,
    prefix_keys,
    cached_prefix_values,
    request_lengths,
    moe_gain,
    expert_ids,
    route_weights,
    w_gate,
    w_up,
    w_down,
):
    tok_count = lax.axis_size("tok")
    grp_count = lax.axis_size("grp")
    tok_rank = lax.axis_index("tok")
    head_rank = lax.axis_index("head")
    tok_dev = hidden_in.shape[1]
    model_width = attn_gain.shape[0]
    head_dim = prefix_keys.shape[3]
    kv_local = prefix_keys.shape[2]
    group_length = w_query.shape[1] // (kv_local * head_dim)
    prefix_total = prefix_keys.shape[1] * tok_count
    quarter = hidden_in[0]
    features = lax.all_gather(quarter, "head", axis=1, tiled=True)
    attention_input = rms_norm(features, attn_gain)
    lengths = request_lengths[0]
    request_ends = jnp.cumsum(lengths)
    starts = request_ends - lengths
    token_index = tok_rank * tok_dev + jnp.arange(tok_dev, dtype=jnp.int32)
    own_start = jnp.max(
        jnp.where(starts[None, :] <= token_index[:, None], starts[None, :], 0), axis=1
    )
    token_positions = prefix_total + token_index - own_start
    full_query, full_key, full_value, full_out = (
        lax.all_gather(w_query, "grp", axis=0, tiled=True),
        lax.all_gather(key_projection_weight, "grp", axis=0, tiled=True),
        lax.all_gather(value_projection_weight, "grp", axis=0, tiled=True),
        lax.all_gather(w_out, "grp", axis=0, tiled=True),
    )
    query_product = jnp.dot(attention_input, full_query, preferred_element_type=jnp.float32)
    key_product = jnp.dot(attention_input, full_key, preferred_element_type=jnp.float32)
    value_product = jnp.dot(attention_input, full_value, preferred_element_type=jnp.float32)
    queries = apply_rotary(
        query_product.reshape(tok_dev, kv_local * group_length, head_dim), token_positions
    )
    queries = queries.reshape(tok_dev, kv_local, group_length, head_dim)
    request_suffix_keys = apply_rotary(
        key_product.reshape(tok_dev, kv_local, head_dim), token_positions
    )
    request_suffix_values = value_product.astype(jnp.bfloat16).reshape(tok_dev, kv_local, head_dim)
    running = (
        jnp.full((kv_local, tok_dev, group_length), MASKED, jnp.float32),
        jnp.zeros((kv_local, tok_dev, group_length), jnp.float32),
        jnp.zeros((kv_local, tok_dev, group_length, head_dim), jnp.float32),
    )
    running = attend(
        running,
        queries,
        lax.all_gather(prefix_keys[0], "tok", axis=0, tiled=True),
        lax.all_gather(cached_prefix_values[0], "tok", axis=0, tiled=True),
        None,
    )

    def visible_from(first_index, count):
        key_index = first_index + jnp.arange(count, dtype=jnp.int32)
        return (key_index[None, :] >= own_start[:, None]) & (
            key_index[None, :] <= token_index[:, None]
        )

    running = attend(
        running,
        queries,
        request_suffix_keys,
        request_suffix_values,
        visible_from(tok_rank * tok_dev, tok_dev),
    )
    longest = tok_dev * tok_count // 4
    reach_devices = (longest - 1 + tok_dev - 1) // tok_dev
    stacked = jnp.stack([request_suffix_keys, request_suffix_values])
    for distance in range(1, reach_devices + 1):
        arrived = shifted(stacked, "tok", distance)
        running = attend(
            running,
            queries,
            arrived[0],
            arrived[1],
            visible_from((tok_rank - distance) * tok_dev, tok_dev),
        )
    row_max, row_total, summed = running
    attended = (summed / row_total[..., None]).astype(jnp.bfloat16)
    attended = jnp.transpose(attended, (1, 0, 2, 3)).reshape(
        tok_dev, kv_local * group_length * head_dim
    )
    partial_value = lax.dot_general(
        attended, full_out, (((1,), (1,)), ((), ())), preferred_element_type=jnp.float32
    )
    share_width = model_width // lax.axis_size("head")
    mixed_sum = lax.psum(partial_value.astype(jnp.bfloat16), "head").astype(jnp.float32)
    mid_full = (features.astype(jnp.float32) + mixed_sum).astype(jnp.bfloat16)
    mid_quarter = lax.dynamic_slice_in_dim(mid_full, head_rank * share_width, share_width, 1)
    moe_in = rms_norm(mid_full, moe_gain)
    experts = grp_count * tok_count * w_gate.shape[0]
    top_count = expert_ids.shape[2]
    capacity = 4 * tok_dev * top_count // (3 * experts)
    chosen = expert_ids[0].reshape(-1)
    onehot = (chosen[:, None] == jnp.arange(experts, dtype=jnp.int32)[None, :]).astype(jnp.int32)
    slot_rank = jnp.sum(onehot * jnp.cumsum(onehot, axis=0), axis=1) - 1
    slot_place = chosen * capacity + slot_rank
    choice_token = jnp.arange(tok_dev * top_count, dtype=jnp.int32) // top_count
    source = jnp.full((experts * capacity,), tok_dev, jnp.int32).at[slot_place].set(choice_token)
    outgoing = jnp.take(moe_in, source, axis=0, mode="fill", fill_value=0).reshape(
        experts, capacity, model_width
    )
    incoming = lax.all_to_all(outgoing, ("grp", "tok"), split_axis=0, concat_axis=0, tiled=True)
    flat_rows = incoming.reshape(-1, model_width)
    gate_act = jnp.dot(flat_rows, w_gate[0], preferred_element_type=jnp.float32)
    up_act = jnp.dot(flat_rows, w_up[0], preferred_element_type=jnp.float32)
    hidden = (jax.nn.silu(gate_act) * up_act).astype(jnp.bfloat16)
    down_rows = w_down[0]
    result = jnp.dot(
        lax.all_gather(hidden, "head", axis=1, tiled=True),
        down_rows,
        preferred_element_type=jnp.float32,
    )
    expert_out = result.astype(jnp.bfloat16).reshape(
        incoming.shape[0], incoming.shape[1], w_down.shape[2]
    )
    returned = lax.all_to_all(expert_out, ("grp", "tok"), split_axis=0, concat_axis=0, tiled=True)
    returned = returned.reshape(experts * capacity, share_width)
    picked = jnp.take(returned, slot_place, axis=0).astype(jnp.float32)
    weighted = jnp.sum(
        (picked * route_weights[0].reshape(-1)[:, None]).reshape(tok_dev, top_count, share_width),
        axis=1,
    )
    output = (mid_quarter.astype(jnp.float32) + weighted).astype(jnp.bfloat16)
    return output[None]


def solution(mesh):
    return jax.shard_map(
        on_device,
        mesh=mesh,
        in_specs=(
            P("grp", "tok", "head"),
            P(),
            P("grp", "head"),
            P("grp", "head"),
            P("grp", "head"),
            P("grp", "head"),
            P("grp", "tok", "head", None),
            P("grp", "tok", "head", None),
            P("grp", None),
            P(),
            P("grp", "tok", None),
            P("grp", "tok", None),
            P(("grp", "tok"), None, "head"),
            P(("grp", "tok"), None, "head"),
            P(("grp", "tok"), None, "head"),
        ),
        out_specs=P("grp", "tok", "head"),
        check_vma=False,
    )
```

profile of v0, /device:TPU:1, one launch (start us, length us, event | category | flops | bytes accessed | tf_op | source)
XLA Modules:
  0.0 505.7 jit_solution(13813160702682913209)
XLA Ops:
  6.5 0.7 all-gather.7.cloned.1.call-update
  7.3 0.7 convert_element_type.128
  8.0 0.8 reduce-window_clone.1
  8.9 0.7 subtract_bitcast_fusion
  9.6 13.2 %all-gather = bf16[1,128,2560]{2,1,0:T(8,128)(2,1)S(1)} all-gather(bf16[1,128,640]{2,1,0:T(8,128)(2,1)} %param.15), channel_id=2, replica_groups=mesh['grp'=2,'tok'=32,'head'=4] {'head'}, dimensions={2}, use_global_device_ids=true | all-gather | bytes 819200 | tf_op jit(solution)/shard_map/all_gather | solution.py:96
  23.1 6.3 %all_gather.28 = bf16[2560,128]{1,0:T(8,128)(2,1)S(1)} all-gather(bf16[1280,128]{1,0:T(8,128)(2,1)S(1)} %copy-done.2), channel_id=1, replica_groups=mesh['grp'=2,'tok'=32,'head'=4] {'grp'}, dimensions={0}, use_global_device_ids=true | all-gather | bytes 983040 | tf_op jit(solution)/shard_map/all_gather | solution.py:108
  29.4 2.3 all_gather.29
  33.0 0.6 pad_maximum_fusion.1
  33.6 1.9 collective-permute-start
  35.5 4.6 collective-permute-start.1
  40.1 4.3 collective-permute-start.2
  44.4 3.6 collective-permute-start.3
  48.0 3.9 collective-permute-start.4
  52.0 1.0 multiply_cosine_fusion
  53.4 0.6 iota_add_fusion
  55.0 0.6 iota_add_fusion.3
  55.6 0.5 iota_add_fusion.4
  57.2 0.6 iota_add_fusion.7
  57.8 39.5 %all-gather.1 = bf16[1,2048,1,128]{3,1,2,0:T(8,128)(2,1)S(1)} all-gather(bf16[1,64,1,128]{3,1,2,0:T(8,128)(2,1)S(1)} %copy-done.19), channel_id=3, replica_groups=mesh['grp'=2,'tok'=32,'head'=4] {'tok'}, dimensions={1}, use_global_device_ids=true | all-gather | bytes 540672 | tf_op jit(solution)/shard_map/all_gather | solution.py:131
  97.3 39.7 %all-gather.2 = bf16[1,2048,1,128]{3,1,2,0:T(8,128)(2,1)} all-gather(bf16[1,64,1,128]{3,1,2,0:T(8,128)(2,1)S(1)} %copy-done.20), channel_id=4, replica_groups=mesh['grp'=2,'tok'=32,'head'=4] {'tok'}, dimensions={1}, use_global_device_ids=true | all-gather | bytes 540672 | tf_op jit(solution)/shard_map/all_gather | solution.py:132
  137.0 0.6 convert_element_type.149
  137.6 1.8 reduce-window.9
  139.9 0.6 broadcast_add_fusion
  140.6 0.7 mul.486
  141.3 1.6 compare_and_fusion.8
  142.9 3.4 fusion.156
  146.3 0.7 fusion.161
  147.0 1.1 copy.185
  148.1 1.8 copy.186
  149.9 1.1 subtract_convert_fusion
  151.2 0.9 multiply_reduce_fusion
  152.1 3.0 collective-permute-start.5
  155.2 1.0 fusion.169
  156.2 4.6 collective-permute-start.6
  160.8 1.0 fusion.168
  161.9 3.4 collective-permute-start.7
  165.2 1.0 fusion.167
  166.3 1.0 fusion.166
  167.3 1.0 fusion.165
  170.1 1.0 fusion
  171.1 1.0 fusion.92
  172.1 1.0 fusion.90
  173.2 1.0 fusion.88
  174.1 1.0 fusion.86
  175.8 1.2 fusion.52
  177.2 1.1 fusion.55
  178.4 4.0 convolution_convert_fusion
  182.5 3.4 scatter_custom_fusion
  186.0 66.5 %all-reduce.2.cloned.1.call-done = bf16[128,2560]{1,0:T(8,128)(2,1)} async-done(((bf16[128,2560]{1,0:T(8,128)(2,1)}), bf16[128,2560]{1,0:T(8,128)(2,1)}) %all-reduce.2.cloned.1.call-update) | async-done | bytes 655376 | tf_op jit(solution)/shard_map/psum | solution.py:170
  252.6 2.2 fusion.17
  254.8 1.3 fusion.19
  256.1 6.3 %gather_fusion = bf16[1024,2560]{1,0:T(8,128)(2,1)} fusion(bf16[128,2560]{1,0:T(8,128)(2,1)S(1)} %fusion.19, s32[1024]{0:T(1024)S(1)} %fusion.138), kind=kCustom, calls=%fused_computation | custom fusion | bytes 10489856 | tf_op jit(solution)/shard_map/jit(_take)/gather | solution.py:183
  262.4 2.9 broadcast_select_fusion
  265.3 130.5 %all_to_all.10 = bf16[64,16,2560]{2,1,0:T(8,128)(2,1)S(1)} all-to-all(bf16[64,16,2560]{2,1,0:T(8,128)(2,1)S(1)} %broadcast_select_fusion), channel_id=1, replica_groups=mesh['grp'=2,'tok'=32,'head'=4] {'grp','tok'}, dimensions={0} | all-to-all | bytes 10485760 | tf_op jit(solution)/shard_map/all_to_all | solution.py:186
  395.8 2.9 fusion.10
  398.7 3.8 multiply_convert_fusion
  402.6 38.6 %all-gather.11.cloned.1.call-done = bf16[1024,1536]{1,0:T(8,128)(2,1)} async-done(((bf16[1024,384]{1,0:T(8,128)(2,1)}), bf16[1024,1536]{1,0:T(8,128)(2,1)}) %all-gather.11.cloned.1.call-update) | async-done | bytes 3145744 | tf_op jit(solution)/shard_map/all_gather | solution.py:193
  441.2 5.6 %fusion.12 = bf16[1024,640]{1,0:T(8,128)(2,1)} fusion(bf16[1024,1536]{1,0:T(8,128)(2,1)} %all-gather.11.cloned.1.call-done, bf16[1,1536,640]{2,1,0:T(8,128)(2,1)S(1)} %copy-done), kind=kOutput, calls=%fused_computation.24 | convolution fusion | flops 2013921280 | bytes 6422528 | tf_op jit(solution)/shard_map/dot_general | solution.py:192
  446.7 10.9 %all-to-all-start.1 = ((bf16[64,16,640]{2,1,0:T(8,128)(2,1)}), bf16[64,16,640]{2,1,0:T(8,128)(2,1)S(1)}, u32[]{:S(2)}, u32[]{:S(2)}) async-start(bf16[64,16,640]{2,1,0:T(8,128)(2,1)} %bitcast.201), calls=%async_computation.1 | async-start | bytes 2621440 | tf_op jit(solution)/shard_map/all_to_all | solution.py:200
  458.2 32.9 %all-to-all-done.1 = bf16[64,16,640]{2,1,0:T(8,128)(2,1)S(1)} async-done(((bf16[64,16,640]{2,1,0:T(8,128)(2,1)}), bf16[64,16,640]{2,1,0:T(8,128)(2,1)S(1)}, u32[]{:S(2)}, u32[]{:S(2)}) %all-to-all-start.1) | async-done | bytes 1310752 | tf_op jit(solution)/shard_map/all_to_all | solution.py:200
  491.0 3.4 gather_fusion.1
  494.4 2.1 gather.15
  496.5 1.0 multiply_reduce_fusion.1
  497.5 1.6 fusion.96
  (125 shorter events, 8.2 us)
Async XLA Ops:
  6.5 434.6 %copy-start = (bf16[1,1536,640]{2,1,0:T(8,128)(2,1)S(1)}, bf16[1,1536,640]{2,1,0:T(8,128)(2,1)}, u32[]{:S(2)}) copy-start(bf16[1,1536,640]{2,1,0:T(8,128)(2,1)} %param.29) | copy-start | bytes 5898244
  6.5 16.6 %copy-start.2 = (bf16[1280,128]{1,0:T(8,128)(2,1)S(1)}, bf16[1280,128]{1,0:T(8,128)(2,1)}, u32[]{:S(2)}) copy-start(bf16[1280,128]{1,0:T(8,128)(2,1)} %param.18) | copy-start | bytes 983044
  6.5 22.8 %copy-start.3 = (bf16[1280,128]{1,0:T(8,128)(2,1)S(1)}, bf16[1280,128]{1,0:T(8,128)(2,1)}, u32[]{:S(2)}) copy-start(bf16[1280,128]{1,0:T(8,128)(2,1)} %param.19) | copy-start | bytes 983044
  6.5 136.4 %all-gather.7.cloned.1.call-start = ((), (), s32[]{:S(2)}) async-start(), calls=%async_computation.2 | async-start | bytes 4915200 | tf_op jit(solution)/shard_map/all_gather | solution.py:107
  7.3 171.2 %all-gather.9.cloned.1.call-start = ((), (), s32[]{:S(2)}) async-start(), calls=%async_computation.3 | async-start | bytes 4915200 | tf_op jit(solution)/shard_map/all_gather | solution.py:110
  8.0 24.4 %copy-start.15 = (f32[2560]{0:T(1024)}, f32[2560]{0:T(1024)S(1)}, u32[]{:S(2)}) copy-start(f32[2560]{0:T(1024)S(1)} %convert_element_type.128) | copy-start | bytes 30724
  8.9 0.7 copy-start.24
  9.6 22.5 %copy-start.25 = (s32[128]{0:T(128)}, s32[128]{0:T(128)S(1)}, u32[]{:S(2)}) copy-start(s32[128]{0:T(128)S(1)} %select_reduce_fusion) | copy-start | bytes 1540
  31.7 20.3 %copy-start.26 = (f32[128]{0:T(128)}, f32[128]{0:T(128)S(1)}, u32[]{:S(2)}) copy-start(f32[128]{0:T(128)S(1)} %add_rsqrt_fusion.1) | copy-start | bytes 1540
  32.2 20.8 %copy-start.17 = (s32[1,128,6]{1,0,2:T(1,128)S(1)}, s32[1,128,6]{1,0,2:T(1,128)}, u32[]{:S(2)}) copy-start(s32[1,128,6]{1,0,2:T(1,128)} %param.25) | copy-start | bytes 9220
  32.2 25.6 %copy-start.19 = (bf16[1,64,1,128]{3,1,2,0:T(8,128)(2,1)S(1)}, bf16[1,64,1,128]{3,1,2,0:T(8,128)(2,1)}, u32[]{:S(2)}) copy-start(bf16[1,64,1,128]{3,1,2,0:T(8,128)(2,1)} %param.21) | copy-start | bytes 49156
  32.4 0.6 copy-start.8
  32.4 1.2 copy-start.10
  32.4 64.8 %copy-start.20 = (bf16[1,64,1,128]{3,1,2,0:T(8,128)(2,1)S(1)}, bf16[1,64,1,128]{3,1,2,0:T(8,128)(2,1)}, u32[]{:S(2)}) copy-start(bf16[1,64,1,128]{3,1,2,0:T(8,128)(2,1)} %param.22) | copy-start | bytes 49156
  32.9 2.6 copy-start.12
  32.9 104.1 %copy-start.22 = (bf16[2560]{0:T(1024)(128)(2,1)S(1)}, bf16[2560]{0:T(1024)(128)(2,1)}, u32[]{:S(2)}) copy-start(bf16[2560]{0:T(1024)(128)(2,1)} %param.24) | copy-start | bytes 15364
  33.6 118.5 %collective-permute-start = (bf16[2,128,1,128]{1,3,2,0:T(8,128)(2,1)}, bf16[2,128,1,128]{1,3,2,0:T(8,128)(2,1)}, u32[]{:S(2)}, u32[]{:S(2)}) collective-permute-start(bf16[2,128,1,128]{1,3,2,0:T(8,128)(2,1)} %pad_maximum_fusion.1), channel_id=1, source_target_pairs={{0,4},{4,8},{8,12},{12,16},{16,20},{20,24},{24,28},{28,32},{32,36}... | collective-permute-start | bytes 196616 | tf_op jit(solution)/shard_map/ppermute | solution.py:15
  35.5 120.7 %collective-permute-start.1 = (bf16[2,128,1,128]{1,3,2,0:T(8,128)(2,1)}, bf16[2,128,1,128]{1,3,2,0:T(8,128)(2,1)}, u32[]{:S(2)}, u32[]{:S(2)}) collective-permute-start(bf16[2,128,1,128]{1,3,2,0:T(8,128)(2,1)} %pad_maximum_fusion.1), channel_id=1, source_target_pairs={{0,8},{4,12},{8,16},{12,20},{16,24},{20,28},{24,32},{28,36},{32,40... | collective-permute-start | bytes 196616 | tf_op jit(solution)/shard_map/ppermute | solution.py:15
  40.1 121.7 %collective-permute-start.2 = (bf16[2,128,1,128]{1,3,2,0:T(8,128)(2,1)}, bf16[2,128,1,128]{1,3,2,0:T(8,128)(2,1)}, u32[]{:S(2)}, u32[]{:S(2)}) collective-permute-start(bf16[2,128,1,128]{1,3,2,0:T(8,128)(2,1)} %pad_maximum_fusion.1), channel_id=1, source_target_pairs={{0,12},{4,16},{8,20},{12,24},{16,28},{20,32},{24,36},{28,40},{32,4... | collective-permute-start | bytes 196616 | tf_op jit(solution)/shard_map/ppermute | solution.py:15
  44.4 121.8 %collective-permute-start.3 = (bf16[2,128,1,128]{1,3,2,0:T(8,128)(2,1)}, bf16[2,128,1,128]{1,3,2,0:T(8,128)(2,1)}, u32[]{:S(2)}, u32[]{:S(2)}) collective-permute-start(bf16[2,128,1,128]{1,3,2,0:T(8,128)(2,1)} %pad_maximum_fusion.1), channel_id=1, source_target_pairs={{0,16},{4,20},{8,24},{12,28},{16,32},{20,36},{24,40},{28,44},{32,4... | collective-permute-start | bytes 196616 | tf_op jit(solution)/shard_map/ppermute | solution.py:15
  48.0 119.3 %collective-permute-start.4 = (bf16[2,128,1,128]{1,3,2,0:T(8,128)(2,1)}, bf16[2,128,1,128]{1,3,2,0:T(8,128)(2,1)}, u32[]{:S(2)}, u32[]{:S(2)}) collective-permute-start(bf16[2,128,1,128]{1,3,2,0:T(8,128)(2,1)} %pad_maximum_fusion.1), channel_id=1, source_target_pairs={{0,20},{4,24},{8,28},{12,32},{16,36},{20,40},{24,44},{28,48},{32,5... | collective-permute-start | bytes 196616 | tf_op jit(solution)/shard_map/ppermute | solution.py:15
  52.0 200.6 %all-reduce.2.cloned.1.call-start = ((), (), s32[]{:S(2)}) async-start(), calls=%async_computation.4 | async-start | bytes 1310720 | tf_op jit(solution)/shard_map/psum | solution.py:170
  151.1 9.7 %copy-start.7 = (pred[128,128]{0,1:T(8,128)(4,1)S(1)}, pred[128,128]{0,1:T(8,128)(4,1)}, u32[]{:S(2)}) copy-start(pred[128,128]{0,1:T(8,128)(4,1)} %get-tuple-element.42) | copy-start | bytes 49156
  151.2 14.1 %copy-start.6 = (pred[128,128]{0,1:T(8,128)(4,1)S(1)}, pred[128,128]{0,1:T(8,128)(4,1)}, u32[]{:S(2)}) copy-start(pred[128,128]{0,1:T(8,128)(4,1)} %get-tuple-element.35) | copy-start | bytes 49156
  151.2 15.1 %copy-start.5 = (pred[128,128]{0,1:T(8,128)(4,1)S(1)}, pred[128,128]{0,1:T(8,128)(4,1)}, u32[]{:S(2)}) copy-start(pred[128,128]{0,1:T(8,128)(4,1)} %get-tuple-element.36) | copy-start | bytes 49156
  152.1 15.2 %copy-start.4 = (pred[128,128]{0,1:T(8,128)(4,1)S(1)}, pred[128,128]{0,1:T(8,128)(4,1)}, u32[]{:S(2)}) copy-start(pred[128,128]{0,1:T(8,128)(4,1)} %get-tuple-element.37) | copy-start | bytes 49156
  152.1 16.8 %copy-start.9 = (bf16[128,1,64]{0,2,1:T(8,128)(2,1)S(1)}, bf16[128,1,64]{0,2,1:T(8,128)(2,1)}, u32[]{:S(2)}) copy-start(bf16[128,1,64]{0,2,1:T(8,128)(2,1)} %copy-done.8) | copy-start | bytes 49156
  152.1 16.8 %copy-start.11 = (bf16[128,1,64]{0,2,1:T(8,128)(2,1)S(1)}, bf16[128,1,64]{0,2,1:T(8,128)(2,1)}, u32[]{:S(2)}) copy-start(bf16[128,1,64]{0,2,1:T(8,128)(2,1)} %copy-done.10) | copy-start | bytes 49156
  152.1 16.2 %collective-permute-start.5 = (bf16[2,128,1,128]{1,3,2,0:T(8,128)(2,1)}, bf16[2,128,1,128]{1,3,2,0:T(8,128)(2,1)S(1)}, u32[]{:S(2)}, u32[]{:S(2)}) collective-permute-start(bf16[2,128,1,128]{1,3,2,0:T(8,128)(2,1)} %pad_maximum_fusion.1), channel_id=1, source_target_pairs={{0,24},{4,28},{8,32},{12,36},{16,40},{20,44},{24,48},{28,52},{32,5... | collective-permute-start | bytes 196616 | tf_op jit(solution)/shard_map/ppermute | solution.py:15
  156.2 12.4 %collective-permute-start.6 = (bf16[2,128,1,128]{1,3,2,0:T(8,128)(2,1)}, bf16[2,128,1,128]{1,3,2,0:T(8,128)(2,1)S(1)}, u32[]{:S(2)}, u32[]{:S(2)}) collective-permute-start(bf16[2,128,1,128]{1,3,2,0:T(8,128)(2,1)} %pad_maximum_fusion.1), channel_id=1, source_target_pairs={{0,28},{4,32},{8,36},{12,40},{16,44},{20,48},{24,52},{28,56},{32,6... | collective-permute-start | bytes 196616 | tf_op jit(solution)/shard_map/ppermute | solution.py:15
  161.9 7.3 %collective-permute-start.7 = (bf16[2,128,1,128]{1,3,2,0:T(8,128)(2,1)}, bf16[2,128,1,128]{1,3,2,0:T(8,128)(2,1)S(1)}, u32[]{:S(2)}, u32[]{:S(2)}) collective-permute-start(bf16[2,128,1,128]{1,3,2,0:T(8,128)(2,1)} %pad_maximum_fusion.1), channel_id=1, source_target_pairs={{0,32},{4,36},{8,40},{12,44},{16,48},{20,52},{24,56},{28,60},{32,6... | collective-permute-start | bytes 196616 | tf_op jit(solution)/shard_map/ppermute | solution.py:15
  172.1 3.7 copy-start.1
  175.8 1.2 copy-start.13
  178.4 4.1 copy-start.16
  178.4 4.1 copy-start.21
  182.4 72.4 %copy-start.14 = (f32[2560]{0:T(1024)S(1)}, f32[2560]{0:T(1024)}, u32[]{:S(2)}) copy-start(f32[2560]{0:T(1024)} %convert_element_type.149) | copy-start | bytes 30724
  182.4 258.7 %all-gather.11.cloned.1.call-start = ((), (), s32[]{:S(2)}) async-start(), calls=%async_computation.5 | async-start | bytes 3932160 | tf_op jit(solution)/shard_map/all_gather | solution.py:193
  265.3 130.5 %copy-start.27 = (bf16[1,2560,384]{2,1,0:T(8,128)(2,1)S(1)}, bf16[1,2560,384]{2,1,0:T(8,128)(2,1)}, u32[]{:S(2)}) copy-start(bf16[1,2560,384]{2,1,0:T(8,128)(2,1)} %param.27) | copy-start | bytes 5898244
  395.8 2.9 copy-start.28
  446.7 11.1 %copy-start.18 = (s32[1,128,6]{1,0,2:T(1,128)S(1)}, s32[1,128,6]{1,0,2:T(1,128)}, u32[]{:S(2)}) copy-start(s32[1,128,6]{1,0,2:T(1,128)} %param.25) | copy-start | bytes 9220
  446.7 11.3 %copy-start.23 = (f32[1,128,6]{1,0,2:T(1,128)S(1)}, f32[1,128,6]{1,0,2:T(1,128)}, u32[]{:S(2)}) copy-start(f32[1,128,6]{1,0,2:T(1,128)} %param.26) | copy-start | bytes 9220
  446.7 44.3 %all-to-all-start.1 = ((bf16[64,16,640]{2,1,0:T(8,128)(2,1)}), bf16[64,16,640]{2,1,0:T(8,128)(2,1)S(1)}, u32[]{:S(2)}, u32[]{:S(2)}) async-start(bf16[64,16,640]{2,1,0:T(8,128)(2,1)} %bitcast.201), calls=%async_computation.1 | async-start | bytes 2621440 | tf_op jit(solution)/shard_map/all_to_all | solution.py:200
Sparse Core Ops, SparseCore 0:
  9.2 22.2 all-gather.6
  52.1 18.4 all-gather.8
  182.5 69.9 all-reduce.1
  402.7 38.4 all-gather.10
where the time goes:
time: 507 us; the launch traced here: 506 us
  blocking collectives  232 us (46%)
  waiting for transfers between devices  139 us (27%)
  starting transfers between devices  40.3 us (8%)
  matrix products  34.8 us (7%)
  other arithmetic  25.5 us (5%)
  local copies, waits for them, and re-layouts  21 us (4%)
  between operations  13.8 us (3%)
    all_to_all x1, blocking collectives, on_device(): lax.all_to_all(outgoing, ('grp', 'tok'), split_axis=0, concat_axis=0, til...  131 us
    psum x1, waiting for transfers between devices, on_device(): lax.psum(partial_value.astype(jnp.bfloat16), 'head').astype(jnp.float32)  66.5 us
    all_gather x1, blocking collectives, on_device(): lax.all_gather(cached_prefix_values[0], 'tok', axis=0, tiled=True)  39.7 us
    all_gather x1, blocking collectives, on_device(): lax.all_gather(prefix_keys[0], 'tok', axis=0, tiled=True)  39.5 us
    all_gather x1, waiting for transfers between devices, on_device(): lax.all_gather(hidden, 'head', axis=1, tiled=True)  38.6 us
    all_to_all x1, waiting for transfers between devices, on_device(): lax.all_to_all(expert_out, ('grp', 'tok'), split_axis=0, concat_axis=0, t...  32.9 us
    ppermute x8, starting transfers between devices, shifted(): return lax.ppermute(block, axis, route)  29.3 us
    all_gather x1, blocking collectives, on_device(): features = lax.all_gather(quarter, 'head', axis=1, tiled=True)  13.2 us
  transfers between devices with their start and end apart: 13, of which 3 were waited for; matrix products, arithmetic and copies ran while one was open for 9% of the time, Pallas kernels for 0%

commit v1 on v0

--- a/solution.py
+++ b/solution.py
@@ -1,12 +1,22 @@
+import functools
 import math
 import jax
 import jax.numpy as jnp
 from jax import lax
 from jax.sharding import PartitionSpec as P
+from jax.lax import all_gather
 
 ROPE_BASE = 500000.0
 NORM_EPS = 1e-06
 MASKED = -1e30
+
+
+def _build_face(local_array, net_axis):
+    reply = all_gather(local_array, net_axis)
+    return jnp.sum(reply, axis=0)
+
+
+do_columns = functools.partial(_build_face, net_axis="head")
 
 
 def shifted(block, axis, distance):
@@ -167,7 +177,7 @@
         attended, full_out, (((1,), (1,)), ((), ())), preferred_element_type=jnp.float32
     )
     share_width = model_width // lax.axis_size("head")
-    mixed_sum = lax.psum(partial_value.astype(jnp.bfloat16), "head").astype(jnp.float32)
+    mixed_sum = do_columns(partial_value.astype(jnp.bfloat16)).astype(jnp.float32)
     mid_full = (features.astype(jnp.float32) + mixed_sum).astype(jnp.bfloat16)
     mid_quarter = lax.dynamic_slice_in_dim(mid_full, head_rank * share_width, share_width, 1)
     moe_in = rms_norm(mid_full, moe_gain)

time: 507 us -> 487 us (0.961)
  waiting for transfers between devices: 139 us -> 126 us
  other arithmetic: 25.5 us -> 20.3 us
    psum x1 -> x0, waiting for transfers between devices: 66.5 us -> none  [on_device(): lax.psum(partial_value.astype(jnp.bfloat16), 'head').astype(jnp.float32)]
    all_gather x0 -> x1, waiting for transfers between devices: none -> 54.3 us  [_build_face(): reply = all_gather(local_array, net_axis)]
  transfers between devices with their start and end apart: 13 -> 13, of which waited for: 3 -> 3; matrix products, arithmetic and copies ran while one was open for 9% -> 8% of each run, Pallas kernels for 0% -> 0%
where the time goes in v1:
time: 487 us; the launch traced here: 485 us
  blocking collectives  230 us (47%)
  waiting for transfers between devices  126 us (26%)
  starting transfers between devices  40.5 us (8%)
  matrix products  34.7 us (7%)
  local copies, waits for them, and re-layouts  20.4 us (4%)
  other arithmetic  20.3 us (4%)
  between operations  13.8 us (3%)
    all_to_all x1, blocking collectives, on_device(): lax.all_to_all(outgoing, ('grp', 'tok'), split_axis=0, concat_axis=0, til...  129 us
    all_gather x1, waiting for transfers between devices, _build_face(): reply = all_gather(local_array, net_axis)  54.3 us
    all_gather x1, blocking collectives, on_device(): lax.all_gather(cached_prefix_values[0], 'tok', axis=0, tiled=True)  39.8 us
    all_gather x1, blocking collectives, on_device(): lax.all_gather(prefix_keys[0], 'tok', axis=0, tiled=True)  39.5 us
    all_gather x1, waiting for transfers between devices, on_device(): lax.all_gather(hidden, 'head', axis=1, tiled=True)  37.9 us
    all_to_all x1, waiting for transfers between devices, on_device(): lax.all_to_all(expert_out, ('grp', 'tok'), split_axis=0, concat_axis=0, t...  32.9 us
    ppermute x8, starting transfers between devices, shifted(): return lax.ppermute(block, axis, route)  29.5 us
    all_gather x1, blocking collectives, on_device(): features = lax.all_gather(quarter, 'head', axis=1, tiled=True)  13.2 us
  transfers between devices with their start and end apart: 13, of which 3 were waited for; matrix products, arithmetic and copies ran while one was open for 8% of the time, Pallas kernels for 0%

profile of v1, /device:TPU:1, one launch (start us, length us, event | category | flops | bytes accessed | tf_op | source)
XLA Modules:
  0.0 485.4 jit_solution(1072868642635604587)
XLA Ops:
  6.5 0.7 all-gather.9.cloned.1.call-update
  7.3 0.7 convert_element_type.130
  8.0 0.8 reduce-window_clone.1
  8.9 0.7 subtract_bitcast_fusion
  9.6 13.2 %all-gather = bf16[1,128,2560]{2,1,0:T(8,128)(2,1)S(1)} all-gather(bf16[1,128,640]{2,1,0:T(8,128)(2,1)} %param.15), channel_id=2, replica_groups=mesh['grp'=2,'tok'=32,'head'=4] {'head'}, dimensions={2}, use_global_device_ids=true | all-gather | bytes 819200 | tf_op jit(solution)/shard_map/all_gather | solution.py:106
  23.1 6.3 %all_gather.34 = bf16[2560,128]{1,0:T(8,128)(2,1)S(1)} all-gather(bf16[1280,128]{1,0:T(8,128)(2,1)S(1)} %copy-done.2), channel_id=1, replica_groups=mesh['grp'=2,'tok'=32,'head'=4] {'grp'}, dimensions={0}, use_global_device_ids=true | all-gather | bytes 983040 | tf_op jit(solution)/shard_map/all_gather | solution.py:118
  29.3 2.4 all_gather.35
  31.7 0.5 convolution_bitcast_fusion
  32.4 0.4 convolution_convert_fusion.1
  33.0 0.6 pad_maximum_fusion.1
  33.6 1.9 collective-permute-start
  35.5 4.5 collective-permute-start.1
  40.0 4.3 collective-permute-start.2
  44.4 3.6 collective-permute-start.3
  47.9 4.0 collective-permute-start.4
  52.0 1.0 multiply_cosine_fusion
  53.0 39.5 %all-gather.1 = bf16[1,2048,1,128]{3,1,2,0:T(8,128)(2,1)S(1)} all-gather(bf16[1,64,1,128]{3,1,2,0:T(8,128)(2,1)S(1)} %copy-done.15), channel_id=3, replica_groups=mesh['grp'=2,'tok'=32,'head'=4] {'tok'}, dimensions={1}, use_global_device_ids=true | all-gather | bytes 540672 | tf_op jit(solution)/shard_map/all_gather | solution.py:141
  92.5 39.8 %all-gather.2 = bf16[1,2048,1,128]{3,1,2,0:T(8,128)(2,1)} all-gather(bf16[1,64,1,128]{3,1,2,0:T(8,128)(2,1)S(1)} %copy-done.16), channel_id=4, replica_groups=mesh['grp'=2,'tok'=32,'head'=4] {'tok'}, dimensions={1}, use_global_device_ids=true | all-gather | bytes 540672 | tf_op jit(solution)/shard_map/all_gather | solution.py:142
  132.3 0.8 compare_and_fusion.8
  133.1 3.3 fusion.156
  136.4 0.7 fusion.161
  137.2 1.1 copy.185
  138.3 1.8 copy.186
  140.1 1.1 subtract_convert_fusion
  141.4 0.9 multiply_reduce_fusion
  142.3 3.0 collective-permute-start.5
  145.3 1.0 fusion.169
  146.3 4.9 %collective-permute-start.6 = (bf16[2,128,1,128]{1,3,2,0:T(8,128)(2,1)}, bf16[2,128,1,128]{1,3,2,0:T(8,128)(2,1)S(1)}, u32[]{:S(2)}, u32[]{:S(2)}) collective-permute-start(bf16[2,128,1,128]{1,3,2,0:T(8,128)(2,1)} %pad_maximum_fusion.1), channel_id=1, source_target_pairs={{0,28},{4,32},{8,36},{12,40},{16,44},{20,48},{24,52},{28,56},{32,6... | collective-permute-start | bytes 196616 | tf_op jit(solution)/shard_map/ppermute | solution.py:25
  151.3 1.0 fusion.168
  152.3 3.3 collective-permute-start.7
  155.6 1.0 fusion.167
  156.7 1.0 fusion.166
  157.7 1.0 fusion.165
  158.7 0.3 fusion.164
  159.0 0.3 fusion.163
  159.6 0.3 fusion.162
  160.5 1.0 fusion
  161.5 1.0 fusion.92
  162.5 1.0 fusion.90
  163.5 1.0 fusion.88
  164.5 1.0 fusion.86
  166.2 1.2 fusion.52
  167.6 1.1 fusion.55
  168.8 4.0 convolution_convert_fusion
  173.3 1.8 reduce-window.9
  175.1 0.3 slice_reduce_fusion
  175.9 3.4 scatter_custom_fusion
  179.4 54.3 %all-gather.15.cloned.1.call-done = bf16[512,2560]{1,0:T(8,128)(2,1)} async-done(((bf16[128,2560]{1,0:T(8,128)(2,1)}), bf16[512,2560]{1,0:T(8,128)(2,1)}) %all-gather.15.cloned.1.call-update) | async-done | bytes 2621456 | tf_op jit(solution)/shard_map/all_gather | solution.py:15
  233.7 2.2 reduce_sum.149
  235.9 1.1 fusion.17
  237.0 1.3 fusion.19
  238.3 6.3 %gather_fusion = bf16[1024,2560]{1,0:T(8,128)(2,1)} fusion(bf16[128,2560]{1,0:T(8,128)(2,1)S(1)} %fusion.19, s32[1024]{0:T(1024)S(1)} %fusion.138), kind=kCustom, calls=%fused_computation | custom fusion | bytes 10489856 | tf_op jit(solution)/shard_map/jit(_take)/gather | solution.py:193
  244.6 2.9 broadcast_select_fusion
  247.5 128.7 %all_to_all.10 = bf16[64,16,2560]{2,1,0:T(8,128)(2,1)S(1)} all-to-all(bf16[64,16,2560]{2,1,0:T(8,128)(2,1)S(1)} %broadcast_select_fusion), channel_id=1, replica_groups=mesh['grp'=2,'tok'=32,'head'=4] {'grp','tok'}, dimensions={0} | all-to-all | bytes 10485760 | tf_op jit(solution)/shard_map/all_to_all | solution.py:196
  376.2 2.9 fusion.10
  379.1 3.8 multiply_convert_fusion
  382.9 37.9 %all-gather.13.cloned.1.call-done = bf16[1024,1536]{1,0:T(8,128)(2,1)} async-done(((bf16[1024,384]{1,0:T(8,128)(2,1)}), bf16[1024,1536]{1,0:T(8,128)(2,1)}) %all-gather.13.cloned.1.call-update) | async-done | bytes 3145744 | tf_op jit(solution)/shard_map/all_gather | solution.py:203
  420.9 5.6 %fusion.12 = bf16[1024,640]{1,0:T(8,128)(2,1)} fusion(bf16[1024,1536]{1,0:T(8,128)(2,1)} %all-gather.13.cloned.1.call-done, bf16[1,1536,640]{2,1,0:T(8,128)(2,1)S(1)} %copy-done), kind=kOutput, calls=%fused_computation.24 | convolution fusion | flops 2013921280 | bytes 6422528 | tf_op jit(solution)/shard_map/dot_general | solution.py:202
  426.5 10.9 %all-to-all-start.1 = ((bf16[64,16,640]{2,1,0:T(8,128)(2,1)}), bf16[64,16,640]{2,1,0:T(8,128)(2,1)S(1)}, u32[]{:S(2)}, u32[]{:S(2)}) async-start(bf16[64,16,640]{2,1,0:T(8,128)(2,1)} %bitcast.203), calls=%async_computation.1 | async-start | bytes 2621440 | tf_op jit(solution)/shard_map/all_to_all | solution.py:210
  437.9 32.9 %all-to-all-done.1 = bf16[64,16,640]{2,1,0:T(8,128)(2,1)S(1)} async-done(((bf16[64,16,640]{2,1,0:T(8,128)(2,1)}), bf16[64,16,640]{2,1,0:T(8,128)(2,1)S(1)}, u32[]{:S(2)}, u32[]{:S(2)}) %all-to-all-start.1) | async-done | bytes 1310752 | tf_op jit(solution)/shard_map/all_to_all | solution.py:210
  470.8 3.4 gather_fusion.1
  474.2 2.1 gather.15
  476.2 1.0 multiply_reduce_fusion.1
  477.3 1.6 fusion.96
  (110 shorter events, 4.3 us)
Async XLA Ops:
  6.5 414.4 %copy-start = (bf16[1,1536,640]{2,1,0:T(8,128)(2,1)S(1)}, bf16[1,1536,640]{2,1,0:T(8,128)(2,1)}, u32[]{:S(2)}) copy-start(bf16[1,1536,640]{2,1,0:T(8,128)(2,1)} %param.29) | copy-start | bytes 5898244
  6.5 16.5 %copy-start.2 = (bf16[1280,128]{1,0:T(8,128)(2,1)S(1)}, bf16[1280,128]{1,0:T(8,128)(2,1)}, u32[]{:S(2)}) copy-start(bf16[1280,128]{1,0:T(8,128)(2,1)} %param.18) | copy-start | bytes 983044
  6.5 22.8 %copy-start.3 = (bf16[1280,128]{1,0:T(8,128)(2,1)S(1)}, bf16[1280,128]{1,0:T(8,128)(2,1)}, u32[]{:S(2)}) copy-start(bf16[1280,128]{1,0:T(8,128)(2,1)} %param.19) | copy-start | bytes 983044
  6.5 126.6 %all-gather.9.cloned.1.call-start = ((), (), s32[]{:S(2)}) async-start(), calls=%async_computation.2 | async-start | bytes 4915200 | tf_op jit(solution)/shard_map/all_gather | solution.py:117
  7.3 161.5 %all-gather.11.cloned.1.call-start = ((), (), s32[]{:S(2)}) async-start(), calls=%async_computation.3 | async-start | bytes 4915200 | tf_op jit(solution)/shard_map/all_gather | solution.py:120
  32.2 20.9 %copy-start.15 = (bf16[1,64,1,128]{3,1,2,0:T(8,128)(2,1)S(1)}, bf16[1,64,1,128]{3,1,2,0:T(8,128)(2,1)}, u32[]{:S(2)}) copy-start(bf16[1,64,1,128]{3,1,2,0:T(8,128)(2,1)} %param.21) | copy-start | bytes 49156
  32.4 0.6 copy-start.8
  32.4 1.2 copy-start.10
  32.4 60.1 %copy-start.16 = (bf16[1,64,1,128]{3,1,2,0:T(8,128)(2,1)S(1)}, bf16[1,64,1,128]{3,1,2,0:T(8,128)(2,1)}, u32[]{:S(2)}) copy-start(bf16[1,64,1,128]{3,1,2,0:T(8,128)(2,1)} %param.22) | copy-start | bytes 49156
  32.9 2.6 copy-start.12
  33.6 108.7 %collective-permute-start = (bf16[2,128,1,128]{1,3,2,0:T(8,128)(2,1)}, bf16[2,128,1,128]{1,3,2,0:T(8,128)(2,1)}, u32[]{:S(2)}, u32[]{:S(2)}) collective-permute-start(bf16[2,128,1,128]{1,3,2,0:T(8,128)(2,1)} %pad_maximum_fusion.1), channel_id=1, source_target_pairs={{0,4},{4,8},{8,12},{12,16},{16,20},{20,24},{24,28},{28,32},{32,36}... | collective-permute-start | bytes 196616 | tf_op jit(solution)/shard_map/ppermute | solution.py:25
  35.5 110.8 %collective-permute-start.1 = (bf16[2,128,1,128]{1,3,2,0:T(8,128)(2,1)}, bf16[2,128,1,128]{1,3,2,0:T(8,128)(2,1)}, u32[]{:S(2)}, u32[]{:S(2)}) collective-permute-start(bf16[2,128,1,128]{1,3,2,0:T(8,128)(2,1)} %pad_maximum_fusion.1), channel_id=1, source_target_pairs={{0,8},{4,12},{8,16},{12,20},{16,24},{20,28},{24,32},{28,36},{32,40... | collective-permute-start | bytes 196616 | tf_op jit(solution)/shard_map/ppermute | solution.py:25
  40.0 112.3 %collective-permute-start.2 = (bf16[2,128,1,128]{1,3,2,0:T(8,128)(2,1)}, bf16[2,128,1,128]{1,3,2,0:T(8,128)(2,1)}, u32[]{:S(2)}, u32[]{:S(2)}) collective-permute-start(bf16[2,128,1,128]{1,3,2,0:T(8,128)(2,1)} %pad_maximum_fusion.1), channel_id=1, source_target_pairs={{0,12},{4,16},{8,20},{12,24},{16,28},{20,32},{24,36},{28,40},{32,4... | collective-permute-start | bytes 196616 | tf_op jit(solution)/shard_map/ppermute | solution.py:25
  44.4 112.3 %collective-permute-start.3 = (bf16[2,128,1,128]{1,3,2,0:T(8,128)(2,1)}, bf16[2,128,1,128]{1,3,2,0:T(8,128)(2,1)}, u32[]{:S(2)}, u32[]{:S(2)}) collective-permute-start(bf16[2,128,1,128]{1,3,2,0:T(8,128)(2,1)} %pad_maximum_fusion.1), channel_id=1, source_target_pairs={{0,16},{4,20},{8,24},{12,28},{16,32},{20,36},{24,40},{28,44},{32,4... | collective-permute-start | bytes 196616 | tf_op jit(solution)/shard_map/ppermute | solution.py:25
  47.9 109.7 %collective-permute-start.4 = (bf16[2,128,1,128]{1,3,2,0:T(8,128)(2,1)}, bf16[2,128,1,128]{1,3,2,0:T(8,128)(2,1)}, u32[]{:S(2)}, u32[]{:S(2)}) collective-permute-start(bf16[2,128,1,128]{1,3,2,0:T(8,128)(2,1)} %pad_maximum_fusion.1), channel_id=1, source_target_pairs={{0,20},{4,24},{8,28},{12,32},{16,36},{20,40},{24,44},{28,48},{32,5... | collective-permute-start | bytes 196616 | tf_op jit(solution)/shard_map/ppermute | solution.py:25
  51.9 181.7 %all-gather.15.cloned.1.call-start = ((), (), s32[]{:S(2)}) async-start(), calls=%async_computation.5 | async-start | bytes 3276800 | tf_op jit(solution)/shard_map/all_gather | solution.py:15
  141.3 10.0 %copy-start.7 = (pred[128,128]{0,1:T(8,128)(4,1)S(1)}, pred[128,128]{0,1:T(8,128)(4,1)}, u32[]{:S(2)}) copy-start(pred[128,128]{0,1:T(8,128)(4,1)} %get-tuple-element.42) | copy-start | bytes 49156
  141.3 14.3 %copy-start.6 = (pred[128,128]{0,1:T(8,128)(4,1)S(1)}, pred[128,128]{0,1:T(8,128)(4,1)}, u32[]{:S(2)}) copy-start(pred[128,128]{0,1:T(8,128)(4,1)} %get-tuple-element.35) | copy-start | bytes 49156
  141.3 15.3 %copy-start.5 = (pred[128,128]{0,1:T(8,128)(4,1)S(1)}, pred[128,128]{0,1:T(8,128)(4,1)}, u32[]{:S(2)}) copy-start(pred[128,128]{0,1:T(8,128)(4,1)} %get-tuple-element.36) | copy-start | bytes 49156
  142.3 15.4 %copy-start.4 = (pred[128,128]{0,1:T(8,128)(4,1)S(1)}, pred[128,128]{0,1:T(8,128)(4,1)}, u32[]{:S(2)}) copy-start(pred[128,128]{0,1:T(8,128)(4,1)} %get-tuple-element.37) | copy-start | bytes 49156
  142.3 17.0 %copy-start.9 = (bf16[128,1,64]{0,2,1:T(8,128)(2,1)S(1)}, bf16[128,1,64]{0,2,1:T(8,128)(2,1)}, u32[]{:S(2)}) copy-start(bf16[128,1,64]{0,2,1:T(8,128)(2,1)} %copy-done.8) | copy-start | bytes 49156
  142.3 17.0 %copy-start.11 = (bf16[128,1,64]{0,2,1:T(8,128)(2,1)S(1)}, bf16[128,1,64]{0,2,1:T(8,128)(2,1)}, u32[]{:S(2)}) copy-start(bf16[128,1,64]{0,2,1:T(8,128)(2,1)} %copy-done.10) | copy-start | bytes 49156
  142.3 16.4 %collective-permute-start.5 = (bf16[2,128,1,128]{1,3,2,0:T(8,128)(2,1)}, bf16[2,128,1,128]{1,3,2,0:T(8,128)(2,1)S(1)}, u32[]{:S(2)}, u32[]{:S(2)}) collective-permute-start(bf16[2,128,1,128]{1,3,2,0:T(8,128)(2,1)} %pad_maximum_fusion.1), channel_id=1, source_target_pairs={{0,24},{4,28},{8,32},{12,36},{16,40},{20,44},{24,48},{28,52},{32,5... | collective-permute-start | bytes 196616 | tf_op jit(solution)/shard_map/ppermute | solution.py:25
  146.3 12.6 %collective-permute-start.6 = (bf16[2,128,1,128]{1,3,2,0:T(8,128)(2,1)}, bf16[2,128,1,128]{1,3,2,0:T(8,128)(2,1)S(1)}, u32[]{:S(2)}, u32[]{:S(2)}) collective-permute-start(bf16[2,128,1,128]{1,3,2,0:T(8,128)(2,1)} %pad_maximum_fusion.1), channel_id=1, source_target_pairs={{0,28},{4,32},{8,36},{12,40},{16,44},{20,48},{24,52},{28,56},{32,6... | collective-permute-start | bytes 196616 | tf_op jit(solution)/shard_map/ppermute | solution.py:25
  152.3 7.2 %collective-permute-start.7 = (bf16[2,128,1,128]{1,3,2,0:T(8,128)(2,1)}, bf16[2,128,1,128]{1,3,2,0:T(8,128)(2,1)S(1)}, u32[]{:S(2)}, u32[]{:S(2)}) collective-permute-start(bf16[2,128,1,128]{1,3,2,0:T(8,128)(2,1)} %pad_maximum_fusion.1), channel_id=1, source_target_pairs={{0,32},{4,36},{8,40},{12,44},{16,48},{20,52},{24,56},{28,60},{32,6... | collective-permute-start | bytes 196616 | tf_op jit(solution)/shard_map/ppermute | solution.py:25
  162.5 3.7 copy-start.1
  166.2 1.2 copy-start.13
  168.8 4.1 copy-start.14
  168.8 4.5 copy-start.17
  172.8 248.1 %all-gather.13.cloned.1.call-start = ((), (), s32[]{:S(2)}) async-start(), calls=%async_computation.4 | async-start | bytes 3932160 | tf_op jit(solution)/shard_map/all_gather | solution.py:203
  247.5 128.7 %copy-start.19 = (bf16[1,2560,384]{2,1,0:T(8,128)(2,1)S(1)}, bf16[1,2560,384]{2,1,0:T(8,128)(2,1)}, u32[]{:S(2)}) copy-start(bf16[1,2560,384]{2,1,0:T(8,128)(2,1)} %param.27) | copy-start | bytes 5898244
  376.2 2.9 copy-start.20
  426.5 11.3 %copy-start.18 = (f32[1,128,6]{1,0,2:T(1,128)S(1)}, f32[1,128,6]{1,0,2:T(1,128)}, u32[]{:S(2)}) copy-start(f32[1,128,6]{1,0,2:T(1,128)} %param.26) | copy-start | bytes 9220
  426.5 44.3 %all-to-all-start.1 = ((bf16[64,16,640]{2,1,0:T(8,128)(2,1)}), bf16[64,16,640]{2,1,0:T(8,128)(2,1)S(1)}, u32[]{:S(2)}, u32[]{:S(2)}) async-start(bf16[64,16,640]{2,1,0:T(8,128)(2,1)} %bitcast.203), calls=%async_computation.1 | async-start | bytes 2621440 | tf_op jit(solution)/shard_map/all_to_all | solution.py:210
Sparse Core Ops, SparseCore 0:
  9.2 22.2 all-gather.8
  52.0 18.4 all-gather.10
  172.9 60.6 all-gather.14
  383.1 37.7 all-gather.12
